TPU v7x, 32 devices: a whole 2x2x4 slice. The times are simulated.
32 devices in a mesh: dp: 8 (over z, y), tensor: 4 (over x, core).
Axes of the slice: x: 2, y: 2, z: 4, core: 2. Of those that a mesh axis runs over, the one named last changes fastest.
Arguments:
- q_nope: bfloat16 [32, 2, 128, 128], P('dp', None, 'tensor'), parts along dimension 0, may hold values from -6 to 6
- q_rope: bfloat16 [32, 2, 128, 64], P('dp', None, 'tensor'), parts along dimension 0, may hold values from -8 to 8
- w_uk: bfloat16 [128, 128, 512], P('tensor'), may hold values from -0.5 to 0.5
- w_uv: bfloat16 [128, 512, 128], P('tensor'), may hold values from -0.25 to 0.25
- cache_latent: bfloat16 [32, 8192, 512], P('dp', 'tensor'), parts along dimension 0, may hold values from -4 to 4
- cache_rope: bfloat16 [32, 64, 8192], P('dp', None, 'tensor'), parts along dimension 0, may hold values from -14 to 14
- scale_pool: float32 [5, 2048], P(None, ('dp', 'tensor')), parts along dimension 1, may hold values from 0.3 to 3
- block_index: int32 [32, 64], P('dp', 'tensor'), parts along dimension 0, may hold values from 0 to 255, as said below
- lengths: int32 [32], P('dp'), parts along dimension 0, may hold values from 2048 to 8192, as said below
Outputs:
- head_outputs: bfloat16 [32, 2, 128, 128], P('dp', None, 'tensor'), parts along dimension 0
There are 8 independent parts, one for each index of `dp`. A program takes and returns all parts, laid end to end along the dimension named above; an argument that names none is the same for every part. Nothing has to cross between parts.
Inputs may be any that keep to these rules, and one draw needn't show every extreme that they name: `block_index`: every column of the scale table is named by exactly one cache block of the group. `lengths`: in a group of two or more requests, one request is shorter than 4096 and the others are at least 4096 long.
All inputs are finite; a program needn't handle non-finite values.
Results may differ from a plain program's by a relative error of at most 0.012.
Values may be sent and summed in bfloat16 or wider, within the bound.
No kernel may reach another device: no remote copies, remote signals or barrier semaphores. Data moves between devices by JAX's collectives and lax.ppermute only.
A program may use at most 128 MiB of HBM per device.

v0:
```python
import jax
import jax.numpy as jnp
from jax import lax
from jax.sharding import PartitionSpec as P

masked_score = -1e30


def local(q_nope, q_rope, w_uk, w_uv, cache_latent, cache_rope, scale_pool, block_index, lengths):
    requests, new_tokens, local_heads, nope_width = q_nope.shape
    rope_width = q_rope.shape[3]
    latent_width = w_uk.shape[2]
    local_span = cache_latent.shape[1]
    blocks = block_index.shape[1]
    block_width = local_span // blocks
    groups = scale_pool.shape[0]
    query_latent = jnp.einsum(
        "rthn,hnc->rthc", q_nope, w_uk, preferred_element_type=jnp.float32
    ).astype(jnp.bfloat16)
    every_latent, every_rope = (
        lax.all_gather(query_latent, "tensor", axis=2, tiled=True),
        lax.all_gather(q_rope, "tensor", axis=2, tiled=True),
    )
    scale_table = lax.all_gather(scale_pool, "tensor", axis=1, tiled=True)
    picked = jnp.take(scale_table, block_index, axis=1)
    latent_scale = jnp.transpose(picked[: groups - 1], (1, 2, 0))[:, :, None, :, None]
    latent_full = (
        (
            cache_latent.reshape(requests, blocks, block_width, groups - 1, -1).astype(jnp.float32)
            * latent_scale
        )
        .astype(jnp.bfloat16)
        .reshape(cache_latent.shape)
    )
    rope_scale = picked[groups - 1][:, None, :, None]
    rope_full = (
        (
            cache_rope.reshape(requests, rope_width, blocks, block_width).astype(jnp.float32)
            * rope_scale
        )
        .astype(jnp.bfloat16)
        .reshape(cache_rope.shape)
    )
    head_count = every_latent.shape[2]
    row_count = new_tokens * head_count
    latent_rows = every_latent.reshape(requests, row_count, latent_width)
    rope_rows = every_rope.reshape(requests, row_count, rope_width)
    scores = jnp.einsum(
        "rmc,rpc->rmp", latent_rows, latent_full, preferred_element_type=jnp.float32
    ) + jnp.einsum("rmd,rdp->rmp", rope_rows, rope_full, preferred_element_type=jnp.float32)
    scores = scores * (nope_width + rope_width) ** (-0.5)
    positions = lax.axis_index("tensor") * local_span + jnp.arange(local_span, dtype=jnp.int32)
    limits = lengths[:, None] - new_tokens + jnp.arange(new_tokens, dtype=jnp.int32)[None, :]
    allowed = positions[None, None, :] <= limits[:, :, None]
    allowed = jnp.repeat(allowed, head_count, axis=1)
    scores = jnp.where(allowed, scores, masked_score)
    peak_score = lax.pmax(jnp.max(scores, axis=2), "tensor")
    weights = jnp.exp(scores - peak_score[:, :, None])
    totals = jnp.sum(weights, axis=2).reshape(requests, new_tokens, head_count)
    mixture = jnp.einsum(
        "rmp,rpc->rmc",
        weights.astype(jnp.bfloat16),
        latent_full,
        preferred_element_type=jnp.float32,
    )
    mixture = mixture.reshape(requests, new_tokens, head_count, latent_width)
    summed = jnp.sum(
        lax.all_to_all(mixture[None], "tensor", split_axis=3, concat_axis=0, tiled=True), axis=0
    )
    counted = jnp.sum(
        lax.all_to_all(totals[None, ..., None], "tensor", split_axis=3, concat_axis=0, tiled=True),
        axis=0,
    )
    attended = (summed / counted).astype(jnp.bfloat16)
    projected = jnp.einsum("rthc,hcv->rthv", attended, w_uv, preferred_element_type=jnp.float32)
    return projected.astype(jnp.bfloat16)


def solution(mesh):
    placed = (
        P("dp", None, "tensor", None),
        P("dp", None, "tensor", None),
        P("tensor", None, None),
        P("tensor", None, None),
        P("dp", "tensor", None),
        P("dp", None, "tensor"),
        P(None, ("dp", "tensor")),
        P("dp", "tensor"),
        P("dp"),
    )
    return jax.shard_map(
        local, mesh=mesh, in_specs=placed, out_specs=P("dp", None, "tensor", None), check_vma=False
    )
```

profile of v0, /device:TPU:0, one launch (start us, length us, event | category | flops | bytes accessed | tf_op | source)
XLA Modules:
  0.0 150.1 jit_solution(4714893015191266000)
XLA Ops:
  6.5 0.0 copy-start
  6.5 0.0 all-gather.3.cloned.1.call-start
  6.5 0.8 copy-done
  7.4 3.5 %fusion.14 = bf16[4,2,32,512]{3,0,1,2:T(4,128)(2,1)} fusion(bf16[32,128,512]{2,1,0:T(8,128)(2,1)} %param.11, bf16[4,2,32,128]{3,2,1,0:T(8,128)(2,1)S(1)} %copy-done), kind=kOutput, calls=%fused_computation.16 | convolution fusion | flops 33685504 | bytes 4521984 | tf_op jit(solution)/shard_map/rthn,hnc->rthc/dot_general | solution.py:17
  10.9 0.0 all-gather.3.cloned.1.call-update
  10.9 0.7 compare_select_fusion
  11.6 0.7 compare_and_fusion
  12.3 6.4 %all-gather = f32[4,64,5]{1,2,0:T(8,128)S(1)} all-gather(f32[1,64,5]{1,2,0:T(8,128)} %bitcast.68), channel_id=1, replica_groups=mesh['dp'=8,'tensor'=4] {'tensor'}, dimensions={0}, use_global_device_ids=true | all-gather | bytes 6400 | tf_op jit(solution)/shard_map/all_gather | solution.py:24
  18.7 0.1 copy.50
  18.8 0.1 reshape.58
  18.9 0.6 gather_fusion
  19.5 0.1 copy.51
  19.6 0.1 copy.52
  19.7 6.1 %mul.36 = f32[4,16,128,4,128]{4,3,2,1,0:T(4,128)} broadcast(f32[4,16,4]{2,1,0:T(8,128)S(1)} %copy.52), dimensions={0,1,3} | broadcast | bytes 16778240 | tf_op jit(solution)/shard_map/mul | solution.py:29
  25.8 19.9 %mul.37 = f32[4,2048,512]{2,1,0:T(8,128)} reshape(f32[4,16,128,4,128]{4,3,2,1,0:T(4,128)} %mul.36) | data formatting | bytes 33554432 | tf_op jit(solution)/shard_map/mul | solution.py:29
  45.8 0.1 broadcast_bitcast_fusion
  45.9 0.0 copy-done.3
  45.9 6.2 %all_gather.11 = bf16[4,2,128,64]{3,2,1,0:T(8,128)(2,1)S(1)} all-gather(bf16[4,2,32,64]{3,2,1,0:T(8,128)(2,1)S(1)} %copy-done.3), channel_id=1, replica_groups=mesh['dp'=8,'tensor'=4] {'tensor'}, dimensions={2}, use_global_device_ids=true | all-gather | bytes 163840 | tf_op jit(solution)/shard_map/all_gather | solution.py:22
  52.1 0.0 copy-done.4
  52.1 0.1 iota_add_fusion.1
  52.2 0.1 broadcast_compare_fusion
  52.3 0.0 all-gather.3.cloned.1.call-done
  52.3 1.5 %copy.49 = bf16[4,2,128,512]{3,2,1,0:T(8,128)(2,1)S(1)} copy(bf16[4,2,128,512]{3,0,1,2:T(4,128)(2,1)} %all-gather.3.cloned.1.call-done) | data formatting | bytes 2097152 | tf_op jit(solution)/shard_map/all_gather | solution.py:21
  53.8 0.0 copy-start.2
  53.9 13.8 %fusion.27 = f32[4,256,2048]{2,1,0:T(8,128)} fusion(bf16[4,256,512]{2,1,0:T(8,128)(2,1)S(1)} %bitcast.60, f32[4,2048,512]{2,1,0:T(8,128)} %mul.37, bf16[4,2048,512]{2,1,0:T(8,128)(2,1)} %param.13), kind=kOutput, calls=%fused_computation.36 | convolution fusion | flops 2160066560 | bytes 34603008 | tf_op jit(solution)/shard_map/rmc,rpc->rmp/dot_general | solution.py:48
  67.7 0.0 copy-done.2
  67.7 8.6 %fusion.28 = (f32[4,256]{1,0:T(4,128)S(1)}, f32[4,256,2048]{2,1,0:T(8,128)}) fusion(f32[4,256,2048]{2,1,0:T(8,128)} %fusion.27, bf16[4,256,64]{2,1,0:T(8,128)(2,1)S(1)} %bitcast.61, bf16[4,64,2048]{2,1,0:T(8,128)(2,1)S(1)} %copy-done.2, f32[4,2048]{1,0:T(4,128)S(1)} %bitcast.65, pred[4,2,2048]{2,1,0:T(4,128)(4,1)S(1)} %broadcast_compare_fusion), kind=kOutput, calls=%fused_computation.37 | convolution fusion | flops 278395904 | bytes 18010112 | tf_op jit(solution)/shard_map/rmd,rdp->rmp/dot_general | solution.py:50
  76.3 7.2 %pmax.7 = f32[4,256]{1,0:T(4,128)S(1)} all-reduce(f32[4,256]{1,0:T(4,128)S(1)} %get-tuple-element.5), channel_id=1, replica_groups=mesh['dp'=8,'tensor'=4] {'tensor'}, use_global_device_ids=true, to_apply=%region_1.2 | all-reduce | flops 1024 | bytes 8192 | tf_op jit(solution)/shard_map/pmax | solution.py:57
  83.4 4.6 %fusion.2 = f32[4,256]{1,0:T(4,128)S(1)} fusion(f32[4,256,2048]{2,1,0:T(8,128)} %get-tuple-element.6, f32[4,256]{1,0:T(4,128)S(1)} %pmax.7), kind=kLoop, calls=%fused_computation.6 | loop fusion | flops 4193280 | bytes 8396800 | tf_op jit(solution)/shard_map/reduce_sum | solution.py:59
  88.1 0.2 copy.57
  88.2 0.8 reshape.70
  89.0 3.4 %all-to-all-start.1 = ((f32[4,1,256]{2,1,0:T(1,128)}), f32[4,1,256]{2,1,0:T(1,128)S(1)}, u32[]{:S(2)}, u32[]{:S(2)}) async-start(f32[4,1,256]{2,1,0:T(1,128)} %reshape.70), calls=%async_computation.1 | async-start | bytes 8192 | tf_op jit(solution)/shard_map/all_to_all | solution.py:71
  92.5 13.0 %fusion.4 = f32[4,256,512]{2,1,0:T(8,128)S(1)} fusion(f32[4,256,2048]{2,1,0:T(8,128)} %get-tuple-element.6, f32[4,256]{1,0:T(4,128)S(1)} %pmax.7, f32[4,2048,512]{2,1,0:T(8,128)} %mul.37, bf16[4,2048,512]{2,1,0:T(8,128)(2,1)} %param.13), kind=kOutput, calls=%fused_computation.8 | convolution fusion | flops 2164260864 | bytes 35655680 | tf_op jit(solution)/shard_map/rmp,rpc->rmc/dot_general | solution.py:60
  105.5 0.0 copy-start.1
  105.5 3.0 %copy.55 = f32[1,4,2,128,512]{4,2,1,0,3:T(2,128)} copy(f32[1,4,2,128,512]{4,3,2,1,0:T(8,128)S(1)} %bitcast.58) | data formatting | bytes 4194304 | tf_op jit(solution)/shard_map/broadcast_in_dim;reshape | solution.py:68
  108.5 0.0 all-to-all-done.1
  108.5 3.6 %all-to-all-start = ((f32[1,4,2,128,512]{4,2,1,0,3:T(2,128)}), f32[1,4,2,128,512]{4,2,1,0,3:T(2,128)S(1)}, u32[]{:S(2)}, u32[]{:S(2)}) async-start(f32[1,4,2,128,512]{4,2,1,0,3:T(2,128)} %copy.55), calls=%async_computation | async-start | bytes 4194304 | tf_op jit(solution)/shard_map/all_to_all | solution.py:68
  112.1 0.5 broadcast.43
  112.6 0.7 reduce.7
  113.3 0.2 reshape.71
  113.6 0.1 reduce_sum.29
  113.6 0.1 copy.59
  113.7 24.0 %all-to-all-done = f32[1,4,2,128,512]{4,2,1,0,3:T(2,128)S(1)} async-done(((f32[1,4,2,128,512]{4,2,1,0,3:T(2,128)}), f32[1,4,2,128,512]{4,2,1,0,3:T(2,128)S(1)}, u32[]{:S(2)}, u32[]{:S(2)}) %all-to-all-start) | async-done | bytes 2097184 | tf_op jit(solution)/shard_map/all_to_all | solution.py:68
  137.8 1.5 %reduce_sum.27 = f32[4,2,32,512]{3,1,0,2:T(2,128)S(1)} reduce(f32[4,2,4,32,512]{4,1,0,3,2:T(2,128)S(1)} %bitcast.59, f32[]{:T(128)} %constant.32.clone.1), dimensions={2}, to_apply=%region_2.3 | reduce | flops 393216 | bytes 2621444 | tf_op jit(solution)/shard_map/reduce_sum | solution.py:67
  139.3 0.3 fusion.24
  139.6 3.0 %fusion.20 = bf16[4,2,32,128]{3,0,1,2:T(4,128)(2,1)S(1)} fusion(bf16[32,512,128]{2,1,0:T(8,128)(2,1)} %param.12, bf16[4,2,32,512]{3,2,1,0:T(8,128)(2,1)S(1)} %fusion.24), kind=kOutput, calls=%fused_computation.18 | convolution fusion | flops 33587200 | bytes 4521984 | tf_op jit(solution)/shard_map/rthc,hcv->rthv/dot_general | solution.py:75
  142.6 0.7 copy.61
  143.2 0.0 copy-done.1
  (9 shorter events, 0.0 us)
Async XLA Ops:
  6.5 0.8 copy-start
  6.5 45.8 %all-gather.3.cloned.1.call-start = ((), (), s32[]{:S(2)}) async-start(), calls=%async_computation.2 | async-start | bytes 1310720 | tf_op jit(solution)/shard_map/all_gather | solution.py:21
  25.8 20.1 %copy-start.3 = (bf16[4,2,32,64]{3,2,1,0:T(8,128)(2,1)S(1)}, bf16[4,2,32,64]{3,2,1,0:T(8,128)(2,1)}, u32[]{:S(2)}) copy-start(bf16[4,2,32,64]{3,2,1,0:T(8,128)(2,1)} %param.10) | copy-start | bytes 98308
  25.8 26.3 %copy-start.4 = (s32[4]{0:T(128)S(1)}, s32[4]{0:T(128)}, u32[]{:S(2)}) copy-start(s32[4]{0:T(128)} %param.17) | copy-start | bytes 52
  53.8 13.9 %copy-start.2 = (bf16[4,64,2048]{2,1,0:T(8,128)(2,1)S(1)}, bf16[4,64,2048]{2,1,0:T(8,128)(2,1)}, u32[]{:S(2)}) copy-start(bf16[4,64,2048]{2,1,0:T(8,128)(2,1)} %param.14) | copy-start | bytes 3145732
  89.0 19.5 %all-to-all-start.1 = ((f32[4,1,256]{2,1,0:T(1,128)}), f32[4,1,256]{2,1,0:T(1,128)S(1)}, u32[]{:S(2)}, u32[]{:S(2)}) async-start(f32[4,1,256]{2,1,0:T(1,128)} %reshape.70), calls=%async_computation.1 | async-start | bytes 8192 | tf_op jit(solution)/shard_map/all_to_all | solution.py:71
  105.5 37.7 %copy-start.1 = (bf16[4,2,32,128]{3,2,1,0:T(8,128)(2,1)S(1)}, bf16[4,2,32,128]{3,2,1,0:T(8,128)(2,1)}, u32[]{:S(2)}) copy-start(bf16[4,2,32,128]{3,2,1,0:T(8,128)(2,1)} %param.9) | copy-start | bytes 196612
  108.5 29.2 %all-to-all-start = ((f32[1,4,2,128,512]{4,2,1,0,3:T(2,128)}), f32[1,4,2,128,512]{4,2,1,0,3:T(2,128)S(1)}, u32[]{:S(2)}, u32[]{:S(2)}) async-start(f32[1,4,2,128,512]{4,2,1,0,3:T(2,128)} %copy.55), calls=%async_computation | async-start | bytes 4194304 | tf_op jit(solution)/shard_map/all_to_all | solution.py:68
Sparse Core Ops, SparseCore 0:
  11.1 19.4 all-gather.2
where the time goes:
time: 151 us; the launch traced here: 150 us
  matrix products  42 us (28%)
  local copies, waits for them, and re-layouts  35 us (23%)
  waiting for transfers between devices  24.1 us (16%)
  blocking collectives  19.7 us (13%)
  between operations  13.5 us (9%)
  other arithmetic  8.79 us (6%)
  starting transfers between devices  7.04 us (5%)
    mul x2, local copies, waits for them, and re-layouts, local(): cache_latent.reshape(requests, blocks, block_width, groups - 1, -1)  26 us
    all_to_all x1, waiting for transfers between devices, local(): lax.all_to_all(mixture[None], 'tensor', split_axis=3, concat_axis=0, tile...  24 us
    dot_general x1, matrix products, local(): jnp.einsum('rmc,rpc->rmp', latent_rows, latent_full, preferred_element_ty...  13.8 us
    dot_general x1, matrix products, local(): jnp.einsum('rmp,rpc->rmc', weights.astype(jnp.bfloat16), latent_full, pre...  13 us
    dot_general x1, matrix products, local(): jnp.einsum('rmd,rdp->rmp', rope_rows, rope_full, preferred_element_type=j...  8.56 us
    pmax x1, blocking collectives, local(): peak_score = lax.pmax(jnp.max(scores, axis=2), 'tensor')  7.16 us
    all_gather x1, blocking collectives, local(): scale_table = lax.all_gather(scale_pool, 'tensor', axis=1, tiled=True)  6.36 us
    all_gather x1, blocking collectives, local(): lax.all_gather(q_rope, 'tensor', axis=2, tiled=True)  6.21 us
  transfers between devices with their start and end apart: 3, of which 1 were waited for; matrix products, arithmetic and copies ran while one was open for 31% of the time, Pallas kernels for 0%

commit v1 on v0

v1 whole, which is shorter than its diff:
```python
import functools
import math

import jax
import jax.numpy as jnp
from jax import lax
from jax.experimental import pallas as pl
from jax.experimental.pallas import tpu as pltpu
from jax.sharding import PartitionSpec as P

f32, bf16 = jnp.float32, jnp.bfloat16
masked_score = -1e30
VMEM = pl.BlockSpec(memory_space=pltpu.VMEM)
SMEM = pl.BlockSpec(memory_space=pltpu.SMEM)
HBM = pl.BlockSpec(memory_space=pl.ANY)


def prepare_kernel(
    index_ref, scale_ref, latent_hbm, rope_hbm, key_ref, turned_ref, latent, rope, latent_sem, rope_sem
):
    requests, span, width = latent.shape
    blocks = index_ref.shape[1]
    shards, groups, per = scale_ref.shape
    block = span // blocks
    lanes = width // (groups - 1)
    me = lax.axis_index("tensor")

    def copies(r):
        return (
            pltpu.make_async_copy(latent_hbm.at[r], latent.at[r], latent_sem.at[r]),
            pltpu.make_async_copy(rope_hbm.at[r], rope.at[r], rope_sem.at[r]),
        )

    for r in range(requests):
        for copy in copies(r):
            copy.start()

    def one(r, carry):
        for copy in copies(r):
            copy.wait()
        for b in range(blocks):
            column = index_ref[r, b]
            owner, place = lax.div(column, per), lax.rem(column, per)
            shard = lax.rem(me - owner + shards, shards)
            at = pl.ds(b * block, block)
            for g in range(groups - 1):
                part = pl.ds(g * lanes, lanes)
                scaled = (latent[r, at, part].astype(f32) * scale_ref[shard, g, place]).astype(bf16)
                key_ref[r, at, part] = scaled
                turned_ref[r, part, at] = scaled.T
            turned_ref[r, pl.ds(width, rope.shape[1]), at] = (
                rope[r, :, at].astype(f32) * scale_ref[shard, groups - 1, place]
            ).astype(bf16)
        return carry

    lax.fori_loop(0, requests, one, 0)


def prepare(index, scales, latent, rope):
    requests, span, width = latent.shape
    depth = rope.shape[1]
    return pl.pallas_call(
        prepare_kernel,
        in_specs=[SMEM, SMEM, HBM, HBM],
        out_specs=[VMEM, VMEM],
        out_shape=[
            jax.ShapeDtypeStruct((requests, span, width), bf16),
            jax.ShapeDtypeStruct((requests, width + depth, span), bf16),
        ],
        scratch_shapes=[
            pltpu.VMEM(latent.shape, bf16),
            pltpu.VMEM(rope.shape, bf16),
            pltpu.SemaphoreType.DMA((requests,)),
            pltpu.SemaphoreType.DMA((requests,)),
        ],
        compiler_params=pltpu.CompilerParams(vmem_limit_bytes=34 << 20),
        cost_estimate=pl.CostEstimate(flops=20_000_000, bytes_accessed=20_000_000, transcendentals=0),
        name="prepare",
    )(index, scales, latent, rope)


def attend_kernel(
    tokens, factor, limit_ref, qa_ref, qb_ref, ra_ref, rb_ref, key_ref, turned_ref,
    oa_ref, ob_ref, la_ref, lb_ref,
):
    requests, rows, width = qa_ref.shape
    span = key_ref.shape[1]
    heads = rows // tokens

    def one(r, carry):
        query = jnp.concatenate(
            [
                jnp.concatenate([qa_ref[r], ra_ref[r]], axis=1),
                jnp.concatenate([qb_ref[r], rb_ref[r]], axis=1),
            ],
            axis=0,
        )
        scores = jnp.dot(query, turned_ref[r], preferred_element_type=f32) * factor
        position = lax.broadcasted_iota(jnp.int32, (1, span), 1)
        bias = [
            jnp.where(position <= limit_ref[r] + t, 0.0, masked_score).astype(f32) for t in range(tokens)
        ]
        scores = jnp.concatenate(
            [scores[k * heads : (k + 1) * heads] + bias[k % tokens] for k in range(2 * tokens)], axis=0
        )
        peak = jnp.max(scores, axis=1, keepdims=True)
        weights = jnp.exp2(scores - peak)
        total = jnp.sum(weights, axis=1, keepdims=True)
        mixture = jnp.dot(weights.astype(bf16), key_ref[r], preferred_element_type=f32)
        mixture = (mixture / total).astype(bf16)
        oa_ref[r] = mixture[:rows]
        ob_ref[r] = mixture[rows:]
        level = jnp.broadcast_to(peak + jnp.log2(total), (2 * rows, 128)).T[:1]
        la_ref[r] = level[:, :rows]
        lb_ref[r] = level[:, rows:]
        return carry

    lax.fori_loop(0, requests, one, 0)


def attend(limit, qa, qb, ra, rb, key, turned, tokens, factor):
    requests, rows, width = qa.shape
    span = key.shape[1]
    mixed = jax.ShapeDtypeStruct((requests, rows, width), bf16)
    level = jax.ShapeDtypeStruct((requests, 1, rows), f32)
    return pl.pallas_call(
        functools.partial(attend_kernel, tokens, factor),
        in_specs=[SMEM] + [VMEM] * 6,
        out_specs=[VMEM] * 4,
        out_shape=[mixed, mixed, level, level],
        compiler_params=pltpu.CompilerParams(vmem_limit_bytes=34 << 20),
        cost_estimate=pl.CostEstimate(
            flops=4 * requests * rows * span * (2 * width + 64),
            bytes_accessed=requests * span * width * 2,
            transcendentals=2 * requests * rows * span,
        ),
        name="attend",
    )(limit, qa, qb, ra, rb, key, turned)


def weigh(parts, levels):
    top = functools.reduce(jnp.maximum, levels)
    shares = [jnp.exp2(level - top) for level in levels]
    total = functools.reduce(jnp.add, shares)
    columns = [jnp.swapaxes(share / total, 1, 2) for share in shares]
    joined = functools.reduce(
        jnp.add, [part.astype(f32) * column for part, column in zip(parts, columns)]
    )
    return joined, top + jnp.log2(total)


def local(tensor, q_nope, q_rope, w_uk, w_uv, cache_latent, cache_rope, scale_pool, block_index, lengths):
    requests, tokens, heads, nope_width = q_nope.shape
    rope_width = q_rope.shape[3]
    width = w_uk.shape[2]
    span = cache_latent.shape[1]
    rows = tokens * heads
    chips = tensor // 2
    factor = (nope_width + rope_width) ** -0.5 * math.log2(math.e)

    def move(x, chip, core):
        pairs = [
            (i, 2 * ((i // 2 + chip) % chips) + ((i % 2) ^ core))
            for i in range(tensor)
        ]
        return lax.ppermute(x, "tensor", pairs)

    def shift(x, by):
        return lax.ppermute(x, "tensor", [(i, (i + by) % tensor) for i in range(tensor)])

    rope_rows = q_rope.reshape(requests, rows, rope_width)
    scales = jnp.stack([scale_pool] + [shift(scale_pool, d) for d in range(1, tensor)])
    ropes = {
        (d, k): rope_rows if d == 0 and k == 0 else move(rope_rows, d, k)
        for d in range(chips)
        for k in range(2)
    }
    own = (
        jnp.einsum("rthn,hnc->rthc", q_nope, w_uk, preferred_element_type=f32)
        .astype(bf16)
        .reshape(requests, rows, width)
    )
    queries = {(0, 0): own, (0, 1): move(own, 0, 1)}
    for d in range(1, chips):
        queries[d, 0] = move(own, d, 0)
        queries[d, 1] = move(queries[d, 0], 0, 1)
    key, turned = prepare(block_index, scales, cache_latent, cache_rope)
    limit = lengths - tokens - lax.axis_index("tensor") * span

    parts, levels = [], []
    for d in range(chips):
        oa, ob, la, lb = attend(
            limit, queries[d, 0], queries[d, 1], ropes[d, 0], ropes[d, 1], key, turned, tokens, factor
        )
        ob, lb = move(ob, 0, 1), move(lb, 0, 1)
        if d == 0:
            parts += [oa, ob]
            levels += [la, lb]
        else:
            joined, level = weigh([oa, ob], [la, lb])
            parts.append(move(joined.astype(bf16), -d, 0))
            levels.append(move(level, -d, 0))
    attended, _ = weigh(parts, levels)
    attended = attended.astype(bf16).reshape(requests, tokens, heads, width)
    projected = jnp.einsum("rthc,hcv->rthv", attended, w_uv, preferred_element_type=f32)
    return projected.astype(bf16)


def solution(mesh):
    placed = (
        P("dp", None, "tensor", None),
        P("dp", None, "tensor", None),
        P("tensor", None, None),
        P("tensor", None, None),
        P("dp", "tensor", None),
        P("dp", None, "tensor"),
        P(None, ("dp", "tensor")),
        P("dp", "tensor"),
        P("dp"),
    )
    return jax.shard_map(
        functools.partial(local, mesh.shape["tensor"]),
        mesh=mesh,
        in_specs=placed,
        out_specs=P("dp", None, "tensor", None),
        check_vma=False,
    )
```

time: 151 us -> 54.4 us (0.36)
  matrix products: 42 us -> 3.6 us
  local copies, waits for them, and re-layouts: 35 us -> 8.62 us
  blocking collectives: 19.7 us -> 0 us
  Pallas kernels: 0 us -> 19.1 us
  between operations: 13.5 us -> 0.18 us
  waiting for transfers between devices: 24.1 us -> 11.2 us
  other arithmetic: 8.79 us -> 0.49 us
  starting transfers between devices: 7.04 us -> 11 us
    dot_general x5 -> x2, matrix products: 42 us -> 3.6 us  [the longest x1 2.84 us: local(): jnp.einsum('rthn,hnc->rthc', q_nope, w_uk, preferred_element_type=f32)]
    mul x3 -> x0, local copies, waits for them, and re-layouts: 26 us -> none  [the longest x2 26 us: local(): cache_latent.reshape(requests, blocks, block_width, groups - 1, -1)]
    all_to_all x2 -> x0, waiting for transfers between devices: 24 us -> none  [the longest x1 24 us: local(): lax.all_to_all(mixture[None], 'tensor', split_axis=3, concat_axis=0, tile...]
    pallas_call x0 -> x3, Pallas kernels: none -> 19.1 us  [the longest x2 10.6 us: attend(): pl.pallas_call(functools.partial(attend_kernel, tokens, factor), in_specs...]
    all_gather x2 -> x0, blocking collectives: 12.6 us -> none  [the longest x1 6.36 us: local(): scale_table = lax.all_gather(scale_pool, 'tensor', axis=1, tiled=True)]
    ppermute x0 -> x15, waiting for transfers between devices: none -> 11.2 us  [the longest x12 11.2 us: move(): return lax.ppermute(x, 'tensor', pairs)]
    ppermute x0 -> x15, starting transfers between devices: none -> 11 us  [the longest x12 9.83 us: move(): return lax.ppermute(x, 'tensor', pairs)]
    pmax x1 -> x0, blocking collectives: 7.16 us -> none  [local(): peak_score = lax.pmax(jnp.max(scores, axis=2), 'tensor')]
  transfers between devices with their start and end apart: 3 -> 15, of which waited for: 1 -> 3; matrix products, arithmetic and copies ran while one was open for 31% -> 0% of each run, Pallas kernels for 0% -> 35%
where the time goes in v1:
time: 54.4 us; the launch traced here: 54.2 us
  Pallas kernels  19.1 us (35%)
  waiting for transfers between devices  11.2 us (21%)
  starting transfers between devices  11 us (20%)
  local copies, waits for them, and re-layouts  8.62 us (16%)
  matrix products  3.6 us (7%)
    ppermute x12, waiting for transfers between devices, move(): return lax.ppermute(x, 'tensor', pairs)  11.2 us
    pallas_call x2, Pallas kernels, attend(): pl.pallas_call(functools.partial(attend_kernel, tokens, factor), in_specs...  10.6 us
    ppermute x12, starting transfers between devices, move(): return lax.ppermute(x, 'tensor', pairs)  9.83 us
    pallas_call x1, Pallas kernels, prepare(): pl.pallas_call(prepare_kernel, in_specs=[SMEM, SMEM, HBM, HBM], out_specs...  8.53 us
    unnamed x18, local copies, waits for them, and re-layouts  7.88 us
    dot_general x1, matrix products, local(): jnp.einsum('rthn,hnc->rthc', q_nope, w_uk, preferred_element_type=f32)  2.84 us
    ppermute x3, starting transfers between devices, shift(): lax.ppermute(x, 'tensor', [(i, (i + by) % tensor) for i in range(tensor)])  1.19 us
  transfers between devices with their start and end apart: 15, of which 3 were waited for; matrix products, arithmetic and copies ran while one was open for 0% of the time, Pallas kernels for 35%

profile of v1, /device:TPU:0, one launch (start us, length us, event | category | flops | bytes accessed | tf_op | source)
XLA Modules:
  0.0 54.2 jit_solution(2583373999786893302)
XLA Ops:
  0.0 0.0 copy-start
  0.0 0.0 copy-start.5
  0.0 0.0 copy-start.3
  0.0 0.8 %copy-done = bf16[4,2,32,128]{3,2,1,0:T(8,128)(2,1)S(1)} copy-done((bf16[4,2,32,128]{3,2,1,0:T(8,128)(2,1)S(1)}, bf16[4,2,32,128]{3,2,1,0:T(8,128)(2,1)}, u32[]{:S(2)}) %copy-start) | copy-done | bytes 65560
  0.8 2.8 %fusion.7 = bf16[4,2,32,512]{3,0,1,2:T(4,128)(2,1)S(1)} fusion(bf16[32,128,512]{2,1,0:T(8,128)(2,1)} %param.11, bf16[4,2,32,128]{3,2,1,0:T(8,128)(2,1)S(1)} %copy-done), kind=kOutput, calls=%fused_computation.5 | convolution fusion | flops 33685504 | bytes 4521984 | tf_op jit(solution)/shard_map/rthn,hnc->rthc/dot_general | solution.py:179
  3.7 0.1 copy.11
  3.8 3.0 %collective-permute-start.6 = (bf16[4,64,512]{2,1,0:T(8,128)(2,1)S(1)}, bf16[4,64,512]{2,1,0:T(8,128)(2,1)S(1)}, u32[]{:S(2)}, u32[]{:S(2)}) collective-permute-start(bf16[4,64,512]{2,1,0:T(8,128)(2,1)S(1)} %bitcast.34), channel_id=1, source_target_pairs={{0,2},{1,3},{2,0},{3,1},{4,6},{5,7},{6,4},{7,5},{8,10},{9,11},{10,... | collective-permute-start | bytes 786440 | tf_op jit(solution)/shard_map/ppermute | solution.py:166
  6.8 0.0 collective-permute-start.4
  6.8 1.2 %collective-permute-start.3 = (f32[5,64]{1,0:T(8,128)S(1)}, f32[5,64]{1,0:T(8,128)S(1)}, u32[]{:S(2)}, u32[]{:S(2)}) collective-permute-start(f32[5,64]{1,0:T(8,128)S(1)} %copy-done.7), channel_id=1, source_target_pairs={{0,2},{1,3},{2,0},{3,1},{4,6},{5,7},{6,4},{7,5},{8,10},{9,11},{10,... | collective-permute-start | bytes 3848 | tf_op jit(solution)/shard_map/ppermute | solution.py:169
  8.0 0.0 collective-permute-start.2
  8.0 0.0 copy-done.4
  8.0 1.1 %collective-permute-start.8 = (bf16[4,64,64]{2,1,0:T(8,128)(2,1)S(1)}, bf16[4,64,64]{2,1,0:T(8,128)(2,1)S(1)}, u32[]{:S(2)}, u32[]{:S(2)}) collective-permute-start(bf16[4,64,64]{2,1,0:T(8,128)(2,1)S(1)} %bitcast.37), channel_id=1, source_target_pairs={{0,2},{1,3},{2,0},{3,1},{4,6},{5,7},{6,4},{7,5},{8,10},{9,11},{10,... | collective-permute-start | bytes 98312 | tf_op jit(solution)/shard_map/ppermute | solution.py:166
  9.1 4.8 %collective-permute-done.6.qa_ref = bf16[4,64,512]{2,1,0:T(8,128)(2,1)S(1)} collective-permute-done((bf16[4,64,512]{2,1,0:T(8,128)(2,1)S(1)}, bf16[4,64,512]{2,1,0:T(8,128)(2,1)S(1)}, u32[]{:S(2)}, u32[]{:S(2)}) %collective-permute-start.6) | collective-permute-done | bytes 262176 | tf_op jit(solution)/shard_map/ppermute | solution.py:166
  13.9 0.0 collective-permute-start.7
  13.9 0.0 collective-permute-done.4
  13.9 1.9 %collective-permute-start.9 = (bf16[4,64,64]{2,1,0:T(8,128)(2,1)S(1)}, bf16[4,64,64]{2,1,0:T(8,128)(2,1)S(1)}, u32[]{:S(2)}, u32[]{:S(2)}) collective-permute-start(bf16[4,64,64]{2,1,0:T(8,128)(2,1)S(1)} %bitcast.38), channel_id=1, source_target_pairs={{0,3},{1,2},{2,1},{3,0},{4,7},{5,6},{6,5},{7,4},{8,11},{9,10},{10,... | collective-permute-start | bytes 98312 | tf_op jit(solution)/shard_map/ppermute | solution.py:166
  15.8 0.0 collective-permute-done.3
  15.8 0.0 collective-permute-start
  15.8 0.0 collective-permute-done.2
  15.8 0.5 collective-permute-start.1
  16.4 0.0 copy-start.2
  16.4 3.4 %copy-done.2 = bf16[4,2048,512]{2,1,0:T(8,128)(2,1)S(1)} copy-done((bf16[4,2048,512]{2,1,0:T(8,128)(2,1)S(1)}, bf16[4,2048,512]{2,1,0:T(8,128)(2,1)}, u32[]{:S(2)}) %copy-start.2) | copy-done | bytes 8388632
  19.8 8.5 %prepare.1 = (bf16[4,2048,512]{2,1,0:T(8,128)(2,1)S(1)}, bf16[4,576,2048]{2,1,0:T(8,128)(2,1)}) custom-call(s32[4,16]{1,0:T(4,128)S(1)} %copy-done.5, f32[4,5,64]{2,1,0:T(8,128)S(1)} %pad_maximum_fusion.scale_ref, bf16[4,2048,512]{2,1,0:T(8,128)(2,1)S(1)} %copy-done.2, bf16[4,64,2048]{2,1,0:T(8,128)(2,1)S(1)} %copy-done.3), custom_call_target="tpu_custom_call" | custom-call | flops 20000000 | bytes 20000000 | tf_op jit(solution)/shard_map/prepare/pallas_call | solution.py:62
  28.3 0.0 collective-permute-done.8.ra_ref
  28.3 0.0 collective-permute-done.9.rb_ref
  28.3 0.0 collective-permute-done.7.qb_ref
  28.3 0.0 copy-start.1
  28.3 3.7 %copy-done.1 = bf16[4,576,2048]{2,1,0:T(8,128)(2,1)S(1)} copy-done((bf16[4,576,2048]{2,1,0:T(8,128)(2,1)S(1)}, bf16[4,576,2048]{2,1,0:T(8,128)(2,1)}, u32[]{:S(2)}) %copy-start.1) | copy-done | bytes 9437208
  32.0 5.3 %attend.3 = (bf16[4,64,512]{2,1,0:T(8,128)(2,1)S(1)}, bf16[4,64,512]{2,1,0:T(8,128)(2,1)S(1)}, f32[4,1,64]{2,1,0:T(1,128)S(1)}, f32[4,1,64]{2,1,0:T(1,128)S(1)}) custom-call(s32[4]{0:T(128)S(1)} %add_subtract_fusion.limit_ref, bf16[4,64,512]{2,1,0:T(8,128)(2,1)S(1)} %collective-permute-done.6.qa_ref, bf16[4,64,512]{2,1,0:T(8,128)(2,1)S(1)} %collective-permute-done.7.qb_ref, ...), custom_call_target="tpu_custom_call" | custom-call | flops 2281701376 | bytes 8388608 | tf_op jit(solution)/shard_map/attend/pallas_call | solution.py:126
  37.3 0.1 collective-permute-start.13
  37.4 0.4 collective-permute-start.10
  37.9 0.0 collective-permute-done.1.rb_ref
  37.9 0.0 collective-permute-done.qb_ref
  37.9 5.3 %attend.2 = (bf16[4,64,512]{2,1,0:T(8,128)(2,1)S(1)}, bf16[4,64,512]{2,1,0:T(8,128)(2,1)S(1)}, f32[4,1,64]{2,1,0:T(1,128)S(1)}, f32[4,1,64]{2,1,0:T(1,128)S(1)}) custom-call(s32[4]{0:T(128)S(1)} %add_subtract_fusion.limit_ref, bf16[4,64,512]{2,1,0:T(8,128)(2,1)S(1)} %bitcast.36, bf16[4,64,512]{2,1,0:T(8,128)(2,1)S(1)} %collective-permute-done.qb_ref, ...), custom_call_target="tpu_custom_call" | custom-call | flops 2281701376 | bytes 8388608 | tf_op jit(solution)/shard_map/attend/pallas_call | solution.py:126
  43.2 0.1 collective-permute-start.12
  43.3 0.4 collective-permute-start.5
  43.8 0.0 collective-permute-done.10
  43.8 0.4 collective-permute-start.11
  44.1 0.0 collective-permute-done.13
  44.1 0.2 add_convert_fusion.1
  44.3 1.8 %collective-permute-start.14 = (bf16[4,64,512]{2,1,0:T(8,128)(2,1)S(1)}, bf16[4,64,512]{2,1,0:T(8,128)(2,1)S(1)}, u32[]{:S(2)}, u32[]{:S(2)}) collective-permute-start(bf16[4,64,512]{2,1,0:T(8,128)(2,1)S(1)} %add_convert_fusion.1), channel_id=1, source_target_pairs={{0,2},{1,3},{2,0},{3,1},{4,6},{5,7},{6,4},{7,5},{8,10},{9,11},{10,... | collective-permute-start | bytes 786440 | tf_op jit(solution)/shard_map/ppermute | solution.py:166
  46.1 0.0 collective-permute-done.5
  46.1 1.3 %collective-permute-done.11 = f32[4,1,64]{2,1,0:T(1,128)S(1)} collective-permute-done((f32[4,1,64]{2,1,0:T(1,128)S(1)}, f32[4,1,64]{2,1,0:T(1,128)S(1)}, u32[]{:S(2)}, u32[]{:S(2)}) %collective-permute-start.11) | collective-permute-done | bytes 1056 | tf_op jit(solution)/shard_map/ppermute | solution.py:166
  47.5 0.0 collective-permute-done.12
  47.5 5.0 %collective-permute-done.14 = bf16[4,64,512]{2,1,0:T(8,128)(2,1)S(1)} collective-permute-done((bf16[4,64,512]{2,1,0:T(8,128)(2,1)S(1)}, bf16[4,64,512]{2,1,0:T(8,128)(2,1)S(1)}, u32[]{:S(2)}, u32[]{:S(2)}) %collective-permute-start.14) | collective-permute-done | bytes 262176 | tf_op jit(solution)/shard_map/ppermute | solution.py:166
  52.5 0.2 add_convert_fusion
  52.8 0.8 %fusion.13 = bf16[4,2,32,128]{3,0,1,2:T(4,128)(2,1)S(1)} fusion(bf16[32,512,128]{2,1,0:T(8,128)(2,1)S(1)} %copy-done.6, bf16[4,2,32,512]{3,2,1,0:T(8,128)(2,1)S(1)} %bitcast.41), kind=kOutput, calls=%fused_computation.7 | convolution fusion | flops 33587200 | bytes 4521984 | tf_op jit(solution)/shard_map/rthc,hcv->rthv/dot_general | solution.py:205
  53.6 0.7 %copy.13 = bf16[4,2,32,128]{3,2,1,0:T(8,128)(2,1)} copy(bf16[4,2,32,128]{3,0,1,2:T(4,128)(2,1)S(1)} %fusion.13) | data formatting | bytes 131072 | tf_op jit(solution)/shard_map/convert_element_type | solution.py:206
  (14 shorter events, 0.1 us)
Async XLA Ops:
  0.0 0.8 %copy-start = (bf16[4,2,32,128]{3,2,1,0:T(8,128)(2,1)S(1)}, bf16[4,2,32,128]{3,2,1,0:T(8,128)(2,1)}, u32[]{:S(2)}) copy-start(bf16[4,2,32,128]{3,2,1,0:T(8,128)(2,1)} %param.9) | copy-start | bytes 196612
  0.0 6.8 %copy-start.7 = (f32[5,64]{1,0:T(8,128)S(1)}, f32[5,64]{1,0:T(8,128)}, u32[]{:S(2)}) copy-start(f32[5,64]{1,0:T(8,128)} %param.15) | copy-start | bytes 3844
  0.0 8.0 %copy-start.4 = (bf16[4,2,32,64]{3,2,1,0:T(8,128)(2,1)S(1)}, bf16[4,2,32,64]{3,2,1,0:T(8,128)(2,1)}, u32[]{:S(2)}) copy-start(bf16[4,2,32,64]{3,2,1,0:T(8,128)(2,1)} %param.10) | copy-start | bytes 98308
  0.0 13.9 %copy-start.8 = (s32[4]{0:T(128)S(1)}, s32[4]{0:T(128)}, u32[]{:S(2)}) copy-start(s32[4]{0:T(128)} %param.17) | copy-start | bytes 52
  0.0 16.3 %copy-start.5 = (s32[4,16]{1,0:T(4,128)S(1)}, s32[4,16]{1,0:T(4,128)}, u32[]{:S(2)}) copy-start(s32[4,16]{1,0:T(4,128)} %index_ref.1) | copy-start | bytes 772
  0.0 16.3 %copy-start.3 = (bf16[4,64,2048]{2,1,0:T(8,128)(2,1)S(1)}, bf16[4,64,2048]{2,1,0:T(8,128)(2,1)}, u32[]{:S(2)}) copy-start(bf16[4,64,2048]{2,1,0:T(8,128)(2,1)} %rope_hbm.1) | copy-start | bytes 3145732
  3.8 10.1 %collective-permute-start.6 = (bf16[4,64,512]{2,1,0:T(8,128)(2,1)S(1)}, bf16[4,64,512]{2,1,0:T(8,128)(2,1)S(1)}, u32[]{:S(2)}, u32[]{:S(2)}) collective-permute-start(bf16[4,64,512]{2,1,0:T(8,128)(2,1)S(1)} %bitcast.34), channel_id=1, source_target_pairs={{0,2},{1,3},{2,0},{3,1},{4,6},{5,7},{6,4},{7,5},{8,10},{9,11},{10,... | collective-permute-start | bytes 786440 | tf_op jit(solution)/shard_map/ppermute | solution.py:166
  6.8 7.1 %collective-permute-start.4 = (f32[5,64]{1,0:T(8,128)S(1)}, f32[5,64]{1,0:T(8,128)S(1)}, u32[]{:S(2)}, u32[]{:S(2)}) collective-permute-start(f32[5,64]{1,0:T(8,128)S(1)} %copy-done.7), channel_id=1, source_target_pairs={{0,3},{1,0},{2,1},{3,2},{4,7},{5,4},{6,5},{7,6},{8,11},{9,8},{10,9... | collective-permute-start | bytes 3848 | tf_op jit(solution)/shard_map/ppermute | solution.py:169
  6.8 9.0 %collective-permute-start.3 = (f32[5,64]{1,0:T(8,128)S(1)}, f32[5,64]{1,0:T(8,128)S(1)}, u32[]{:S(2)}, u32[]{:S(2)}) collective-permute-start(f32[5,64]{1,0:T(8,128)S(1)} %copy-done.7), channel_id=1, source_target_pairs={{0,2},{1,3},{2,0},{3,1},{4,6},{5,7},{6,4},{7,5},{8,10},{9,11},{10,... | collective-permute-start | bytes 3848 | tf_op jit(solution)/shard_map/ppermute | solution.py:169
  8.0 7.9 %collective-permute-start.2 = (f32[5,64]{1,0:T(8,128)S(1)}, f32[5,64]{1,0:T(8,128)S(1)}, u32[]{:S(2)}, u32[]{:S(2)}) collective-permute-start(f32[5,64]{1,0:T(8,128)S(1)} %copy-done.7), channel_id=1, source_target_pairs={{0,1},{1,2},{2,3},{3,0},{4,5},{5,6},{6,7},{7,4},{8,9},{9,10},{10,1... | collective-permute-start | bytes 3848 | tf_op jit(solution)/shard_map/ppermute | solution.py:169
  8.0 20.3 %collective-permute-start.8 = (bf16[4,64,64]{2,1,0:T(8,128)(2,1)S(1)}, bf16[4,64,64]{2,1,0:T(8,128)(2,1)S(1)}, u32[]{:S(2)}, u32[]{:S(2)}) collective-permute-start(bf16[4,64,64]{2,1,0:T(8,128)(2,1)S(1)} %bitcast.37), channel_id=1, source_target_pairs={{0,2},{1,3},{2,0},{3,1},{4,6},{5,7},{6,4},{7,5},{8,10},{9,11},{10,... | collective-permute-start | bytes 98312 | tf_op jit(solution)/shard_map/ppermute | solution.py:166
  13.9 14.4 %collective-permute-start.7 = (bf16[4,64,512]{2,1,0:T(8,128)(2,1)S(1)}, bf16[4,64,512]{2,1,0:T(8,128)(2,1)S(1)}, u32[]{:S(2)}, u32[]{:S(2)}) collective-permute-start(bf16[4,64,512]{2,1,0:T(8,128)(2,1)S(1)} %collective-permute-done.6.qa_ref), channel_id=1, source_target_pairs={{0,1},{1,0},{2,3},{3,2},{4,5},{5,4},{6,7},{7,6},{8,9},{9,8},{10,11... | collective-permute-start | bytes 786440 | tf_op jit(solution)/shard_map/ppermute | solution.py:166
  13.9 14.4 %collective-permute-start.9 = (bf16[4,64,64]{2,1,0:T(8,128)(2,1)S(1)}, bf16[4,64,64]{2,1,0:T(8,128)(2,1)S(1)}, u32[]{:S(2)}, u32[]{:S(2)}) collective-permute-start(bf16[4,64,64]{2,1,0:T(8,128)(2,1)S(1)} %bitcast.38), channel_id=1, source_target_pairs={{0,3},{1,2},{2,1},{3,0},{4,7},{5,6},{6,5},{7,4},{8,11},{9,10},{10,... | collective-permute-start | bytes 98312 | tf_op jit(solution)/shard_map/ppermute | solution.py:166
  15.8 22.1 %collective-permute-start = (bf16[4,64,512]{2,1,0:T(8,128)(2,1)S(1)}, bf16[4,64,512]{2,1,0:T(8,128)(2,1)S(1)}, u32[]{:S(2)}, u32[]{:S(2)}) collective-permute-start(bf16[4,64,512]{2,1,0:T(8,128)(2,1)S(1)} %bitcast.35), channel_id=1, source_target_pairs={{0,1},{1,0},{2,3},{3,2},{4,5},{5,4},{6,7},{7,6},{8,9},{9,8},{10,11... | collective-permute-start | bytes 786440 | tf_op jit(solution)/shard_map/ppermute | solution.py:166
  15.8 22.0 %collective-permute-start.1 = (bf16[4,64,64]{2,1,0:T(8,128)(2,1)S(1)}, bf16[4,64,64]{2,1,0:T(8,128)(2,1)S(1)}, u32[]{:S(2)}, u32[]{:S(2)}) collective-permute-start(bf16[4,64,64]{2,1,0:T(8,128)(2,1)S(1)} %bitcast.39), channel_id=1, source_target_pairs={{0,1},{1,0},{2,3},{3,2},{4,5},{5,4},{6,7},{7,6},{8,9},{9,8},{10,11... | collective-permute-start | bytes 98312 | tf_op jit(solution)/shard_map/ppermute | solution.py:166
  16.4 3.4 %copy-start.2 = (bf16[4,2048,512]{2,1,0:T(8,128)(2,1)S(1)}, bf16[4,2048,512]{2,1,0:T(8,128)(2,1)}, u32[]{:S(2)}) copy-start(bf16[4,2048,512]{2,1,0:T(8,128)(2,1)} %latent_hbm.1) | copy-start | bytes 25165828
  28.3 3.7 %copy-start.1 = (bf16[4,576,2048]{2,1,0:T(8,128)(2,1)S(1)}, bf16[4,576,2048]{2,1,0:T(8,128)(2,1)}, u32[]{:S(2)}) copy-start(bf16[4,576,2048]{2,1,0:T(8,128)(2,1)} %get-tuple-element.16.turned_ref) | copy-start | bytes 28311556
  37.3 6.8 %collective-permute-start.13 = (bf16[4,64,512]{2,1,0:T(8,128)(2,1)S(1)}, bf16[4,64,512]{2,1,0:T(8,128)(2,1)S(1)}, u32[]{:S(2)}, u32[]{:S(2)}) collective-permute-start(bf16[4,64,512]{2,1,0:T(8,128)(2,1)S(1)} %get-tuple-element.24), channel_id=1, source_target_pairs={{0,1},{1,0},{2,3},{3,2},{4,5},{5,4},{6,7},{7,6},{8,9},{9,8},{10,11... | collective-permute-start | bytes 786440 | tf_op jit(solution)/shard_map/ppermute | solution.py:166
  37.4 15.3 %copy-start.6 = (bf16[32,512,128]{2,1,0:T(8,128)(2,1)S(1)}, bf16[32,512,128]{2,1,0:T(8,128)(2,1)}, u32[]{:S(2)}) copy-start(bf16[32,512,128]{2,1,0:T(8,128)(2,1)} %param.12) | copy-start | bytes 12582916
  37.4 6.3 %collective-permute-start.10 = (f32[4,1,64]{2,1,0:T(1,128)S(1)}, f32[4,1,64]{2,1,0:T(1,128)S(1)}, u32[]{:S(2)}, u32[]{:S(2)}) collective-permute-start(f32[4,1,64]{2,1,0:T(1,128)S(1)} %get-tuple-element.21), channel_id=1, source_target_pairs={{0,1},{1,0},{2,3},{3,2},{4,5},{5,4},{6,7},{7,6},{8,9},{9,8},{10,11... | collective-permute-start | bytes 3080 | tf_op jit(solution)/shard_map/ppermute | solution.py:166
  43.2 4.3 %collective-permute-start.12 = (bf16[4,64,512]{2,1,0:T(8,128)(2,1)S(1)}, bf16[4,64,512]{2,1,0:T(8,128)(2,1)S(1)}, u32[]{:S(2)}, u32[]{:S(2)}) collective-permute-start(bf16[4,64,512]{2,1,0:T(8,128)(2,1)S(1)} %get-tuple-element.22), channel_id=1, source_target_pairs={{0,1},{1,0},{2,3},{3,2},{4,5},{5,4},{6,7},{7,6},{8,9},{9,8},{10,11... | collective-permute-start | bytes 786440 | tf_op jit(solution)/shard_map/ppermute | solution.py:166
  43.3 2.8 %collective-permute-start.5 = (f32[4,1,64]{2,1,0:T(1,128)S(1)}, f32[4,1,64]{2,1,0:T(1,128)S(1)}, u32[]{:S(2)}, u32[]{:S(2)}) collective-permute-start(f32[4,1,64]{2,1,0:T(1,128)S(1)} %get-tuple-element.19), channel_id=1, source_target_pairs={{0,1},{1,0},{2,3},{3,2},{4,5},{5,4},{6,7},{7,6},{8,9},{9,8},{10,11... | collective-permute-start | bytes 3080 | tf_op jit(solution)/shard_map/ppermute | solution.py:166
  43.8 3.7 %collective-permute-start.11 = (f32[4,1,64]{2,1,0:T(1,128)S(1)}, f32[4,1,64]{2,1,0:T(1,128)S(1)}, u32[]{:S(2)}, u32[]{:S(2)}) collective-permute-start(f32[4,1,64]{2,1,0:T(1,128)S(1)} %get-tuple-element.29), channel_id=1, source_target_pairs={{0,2},{1,3},{2,0},{3,1},{4,6},{5,7},{6,4},{7,5},{8,10},{9,11},{10,... | collective-permute-start | bytes 3080 | tf_op jit(solution)/shard_map/ppermute | solution.py:166
  44.3 8.2 %collective-permute-start.14 = (bf16[4,64,512]{2,1,0:T(8,128)(2,1)S(1)}, bf16[4,64,512]{2,1,0:T(8,128)(2,1)S(1)}, u32[]{:S(2)}, u32[]{:S(2)}) collective-permute-start(bf16[4,64,512]{2,1,0:T(8,128)(2,1)S(1)} %add_convert_fusion.1), channel_id=1, source_target_pairs={{0,2},{1,3},{2,0},{3,1},{4,6},{5,7},{6,4},{7,5},{8,10},{9,11},{10,... | collective-permute-start | bytes 786440 | tf_op jit(solution)/shard_map/ppermute | solution.py:166

commit v2 on v1

--- a/solution.py
+++ b/solution.py
@@ -12,7 +12,7 @@
 masked_score = -1e30
 VMEM = pl.BlockSpec(memory_space=pltpu.VMEM)
 SMEM = pl.BlockSpec(memory_space=pltpu.SMEM)
-HBM = pl.BlockSpec(memory_space=pl.ANY)
+HBM = pl.BlockSpec(memory_space=pltpu.HBM)
 
 
 def prepare_kernel(
@@ -24,6 +24,7 @@
     block = span // blocks
     lanes = width // (groups - 1)
     me = lax.axis_index("tensor")
+    chips = shards // 2
 
     def copies(r):
         return (
@@ -41,7 +42,9 @@
         for b in range(blocks):
             column = index_ref[r, b]
             owner, place = lax.div(column, per), lax.rem(column, per)
-            shard = lax.rem(me - owner + shards, shards)
+            turn = lax.rem(me // 2 - owner // 2 + chips, chips)
+            other = (me - owner) & 1
+            shard = jnp.where(turn == 0, other, turn + 1 + other * (chips - 1))
             at = pl.ds(b * block, block)
             for g in range(groups - 1):
                 part = pl.ds(g * lanes, lanes)
@@ -73,10 +76,15 @@
             pltpu.SemaphoreType.DMA((requests,)),
             pltpu.SemaphoreType.DMA((requests,)),
         ],
-        compiler_params=pltpu.CompilerParams(vmem_limit_bytes=34 << 20),
+        compiler_params=pltpu.CompilerParams(vmem_limit_bytes=14 << 20),
         cost_estimate=pl.CostEstimate(flops=20_000_000, bytes_accessed=20_000_000, transcendentals=0),
         name="prepare",
-    )(index, scales, latent, rope)
+    )(
+        index,
+        scales,
+        pltpu.with_memory_space_constraint(latent, pltpu.HBM),
+        pltpu.with_memory_space_constraint(rope, pltpu.HBM),
+    )
 
 
 def attend_kernel(
@@ -87,7 +95,9 @@
     span = key_ref.shape[1]
     heads = rows // tokens
 
-    def one(r, carry):
+    position = lax.broadcasted_iota(jnp.int32, (1, span), 1)
+
+    def score(r):
         query = jnp.concatenate(
             [
                 jnp.concatenate([qa_ref[r], ra_ref[r]], axis=1),
@@ -95,8 +105,13 @@
             ],
             axis=0,
         )
-        scores = jnp.dot(query, turned_ref[r], preferred_element_type=f32) * factor
-        position = lax.broadcasted_iota(jnp.int32, (1, span), 1)
+        return jnp.dot(query, turned_ref[r], preferred_element_type=f32)
+
+    ahead = score(0)
+    for r in range(requests):
+        scores = ahead * factor
+        if r + 1 < requests:
+            ahead = score(r + 1)
         bias = [
             jnp.where(position <= limit_ref[r] + t, 0.0, masked_score).astype(f32) for t in range(tokens)
         ]
@@ -107,15 +122,12 @@
         weights = jnp.exp2(scores - peak)
         total = jnp.sum(weights, axis=1, keepdims=True)
         mixture = jnp.dot(weights.astype(bf16), key_ref[r], preferred_element_type=f32)
-        mixture = (mixture / total).astype(bf16)
+        mixture = (mixture * (1.0 / total)).astype(bf16)
         oa_ref[r] = mixture[:rows]
         ob_ref[r] = mixture[rows:]
         level = jnp.broadcast_to(peak + jnp.log2(total), (2 * rows, 128)).T[:1]
         la_ref[r] = level[:, :rows]
         lb_ref[r] = level[:, rows:]
-        return carry
-
-    lax.fori_loop(0, requests, one, 0)
 
 
 def attend(limit, qa, qb, ra, rb, key, turned, tokens, factor):
@@ -128,7 +140,7 @@
         in_specs=[SMEM] + [VMEM] * 6,
         out_specs=[VMEM] * 4,
         out_shape=[mixed, mixed, level, level],
-        compiler_params=pltpu.CompilerParams(vmem_limit_bytes=34 << 20),
+        compiler_params=pltpu.CompilerParams(vmem_limit_bytes=14 << 20),
         cost_estimate=pl.CostEstimate(
             flops=4 * requests * rows * span * (2 * width + 64),
             bytes_accessed=requests * span * width * 2,
@@ -165,25 +177,22 @@
         ]
         return lax.ppermute(x, "tensor", pairs)
 
-    def shift(x, by):
-        return lax.ppermute(x, "tensor", [(i, (i + by) % tensor) for i in range(tensor)])
-
-    rope_rows = q_rope.reshape(requests, rows, rope_width)
-    scales = jnp.stack([scale_pool] + [shift(scale_pool, d) for d in range(1, tensor)])
-    ropes = {
-        (d, k): rope_rows if d == 0 and k == 0 else move(rope_rows, d, k)
-        for d in range(chips)
-        for k in range(2)
-    }
+    def spread(x):
+        found = {(0, 0): x, (0, 1): move(x, 0, 1)}
+        for d in range(1, chips):
+            found[d, 0] = move(x, d, 0)
+        for d in range(1, chips):
+            found[d, 1] = move(found[d, 0], 0, 1)
+        return found
+
+    scales = jnp.stack(list(spread(scale_pool).values()))
+    ropes = spread(q_rope.reshape(requests, rows, rope_width))
     own = (
         jnp.einsum("rthn,hnc->rthc", q_nope, w_uk, preferred_element_type=f32)
         .astype(bf16)
         .reshape(requests, rows, width)
     )
-    queries = {(0, 0): own, (0, 1): move(own, 0, 1)}
-    for d in range(1, chips):
-        queries[d, 0] = move(own, d, 0)
-        queries[d, 1] = move(queries[d, 0], 0, 1)
+    queries = spread(own)
     key, turned = prepare(block_index, scales, cache_latent, cache_rope)
     limit = lengths - tokens - lax.axis_index("tensor") * span
 

time: 54.4 us -> 42.6 us (0.78)
  local copies, waits for them, and re-layouts: 8.62 us -> 1.58 us
  Pallas kernels: 19.1 us -> 14.4 us
  waiting for transfers between devices: 11.2 us -> 12.5 us
  starting transfers between devices: 11 us -> 9.75 us
    unnamed x18 -> x12, local copies, waits for them, and re-layouts: 7.88 us -> 0.84 us
    pallas_call x1, Pallas kernels: 8.53 us -> 5.9 us  [prepare(): pl.pallas_call(prepare_kernel, in_specs=[SMEM, SMEM, HBM, HBM], out_specs...]
    pallas_call x2, Pallas kernels: 10.6 us -> 8.54 us  [attend(): pl.pallas_call(functools.partial(attend_kernel, tokens, factor), in_specs...]
    ppermute x12 -> x15, waiting for transfers between devices: 11.2 us -> 12.5 us  [move(): return lax.ppermute(x, 'tensor', pairs)]
    ppermute x3 -> x0, starting transfers between devices: 1.19 us -> none  [shift(): lax.ppermute(x, 'tensor', [(i, (i + by) % tensor) for i in range(tensor)])]
    ppermute x12 -> x15, starting transfers between devices: 9.83 us -> 9.75 us  [move(): return lax.ppermute(x, 'tensor', pairs)]
  transfers between devices with their start and end apart: 15 -> 15, of which waited for: 3 -> 5; matrix products, arithmetic and copies ran while one was open for 0% -> 1% of each run, Pallas kernels for 35% -> 34%
where the time goes in v2:
time: 42.6 us; the launch traced here: 42.4 us
  Pallas kernels  14.4 us (34%)
  waiting for transfers between devices  12.5 us (29%)
  starting transfers between devices  9.75 us (23%)
  matrix products  3.57 us (8%)
  local copies, waits for them, and re-layouts  1.58 us (4%)
  other arithmetic  0.5 us (1%)
    ppermute x15, waiting for transfers between devices, move(): return lax.ppermute(x, 'tensor', pairs)  12.5 us
    ppermute x15, starting transfers between devices, move(): return lax.ppermute(x, 'tensor', pairs)  9.75 us
    pallas_call x2, Pallas kernels, attend(): pl.pallas_call(functools.partial(attend_kernel, tokens, factor), in_specs...  8.54 us
    pallas_call x1, Pallas kernels, prepare(): pl.pallas_call(prepare_kernel, in_specs=[SMEM, SMEM, HBM, HBM], out_specs...  5.9 us
    dot_general x1, matrix products, local(): jnp.einsum('rthn,hnc->rthc', q_nope, w_uk, preferred_element_type=f32)  2.84 us
  transfers between devices with their start and end apart: 15, of which 5 were waited for; matrix products, arithmetic and copies ran while one was open for 1% of the time, Pallas kernels for 34%

profile of v2, /device:TPU:0, one launch (start us, length us, event | category | flops | bytes accessed | tf_op | source)
XLA Modules:
  0.0 42.4 jit_solution(2814210180408798119)
XLA Ops:
  0.0 0.0 copy-start
  0.0 0.0 copy-start.4
  0.0 0.0 copy-start.2
  0.0 0.8 %copy-done = bf16[4,2,32,128]{3,2,1,0:T(8,128)(2,1)S(1)} copy-done((bf16[4,2,32,128]{3,2,1,0:T(8,128)(2,1)S(1)}, bf16[4,2,32,128]{3,2,1,0:T(8,128)(2,1)}, u32[]{:S(2)}) %copy-start) | copy-done | bytes 65560
  0.8 2.8 %fusion.7 = bf16[4,2,32,512]{3,0,1,2:T(4,128)(2,1)S(1)} fusion(bf16[32,128,512]{2,1,0:T(8,128)(2,1)} %param.11, bf16[4,2,32,128]{3,2,1,0:T(8,128)(2,1)S(1)} %copy-done), kind=kOutput, calls=%fused_computation.5 | convolution fusion | flops 33685504 | bytes 4521984 | tf_op jit(solution)/shard_map/rthn,hnc->rthc/dot_general | solution.py:191
  3.7 0.1 copy.11
  3.8 3.0 %collective-permute-start.6 = (bf16[4,64,512]{2,1,0:T(8,128)(2,1)S(1)}, bf16[4,64,512]{2,1,0:T(8,128)(2,1)S(1)}, u32[]{:S(2)}, u32[]{:S(2)}) collective-permute-start(bf16[4,64,512]{2,1,0:T(8,128)(2,1)S(1)} %bitcast.34), channel_id=1, source_target_pairs={{0,2},{1,3},{2,0},{3,1},{4,6},{5,7},{6,4},{7,5},{8,10},{9,11},{10,... | collective-permute-start | bytes 786440 | tf_op jit(solution)/shard_map/ppermute | solution.py:178
  6.8 0.0 copy-done.4
  6.8 0.1 collective-permute-start.3
  6.9 0.0 collective-permute-start.2
  6.9 0.5 %collective-permute-start = (bf16[4,64,512]{2,1,0:T(8,128)(2,1)S(1)}, bf16[4,64,512]{2,1,0:T(8,128)(2,1)S(1)}, u32[]{:S(2)}, u32[]{:S(2)}) collective-permute-start(bf16[4,64,512]{2,1,0:T(8,128)(2,1)S(1)} %bitcast.35), channel_id=1, source_target_pairs={{0,1},{1,0},{2,3},{3,2},{4,5},{5,4},{6,7},{7,6},{8,9},{9,8},{10,11... | collective-permute-start | bytes 786440 | tf_op jit(solution)/shard_map/ppermute | solution.py:178
  7.4 0.0 copy-done.1
  7.4 1.9 %collective-permute-start.8 = (bf16[4,64,64]{2,1,0:T(8,128)(2,1)S(1)}, bf16[4,64,64]{2,1,0:T(8,128)(2,1)S(1)}, u32[]{:S(2)}, u32[]{:S(2)}) collective-permute-start(bf16[4,64,64]{2,1,0:T(8,128)(2,1)S(1)} %bitcast.37), channel_id=1, source_target_pairs={{0,2},{1,3},{2,0},{3,1},{4,6},{5,7},{6,4},{7,5},{8,10},{9,11},{10,... | collective-permute-start | bytes 98312 | tf_op jit(solution)/shard_map/ppermute | solution.py:178
  9.3 4.6 %collective-permute-done.3 = f32[5,64]{1,0:T(8,128)S(1)} collective-permute-done((f32[5,64]{1,0:T(8,128)S(1)}, f32[5,64]{1,0:T(8,128)S(1)}, u32[]{:S(2)}, u32[]{:S(2)}) %collective-permute-start.3) | collective-permute-done | bytes 1312 | tf_op jit(solution)/shard_map/ppermute | solution.py:178
  13.9 0.0 collective-permute-start.4
  13.9 0.0 collective-permute-done.6.qa_ref
  13.9 0.5 %collective-permute-start.7 = (bf16[4,64,512]{2,1,0:T(8,128)(2,1)S(1)}, bf16[4,64,512]{2,1,0:T(8,128)(2,1)S(1)}, u32[]{:S(2)}, u32[]{:S(2)}) collective-permute-start(bf16[4,64,512]{2,1,0:T(8,128)(2,1)S(1)} %collective-permute-done.6.qa_ref), channel_id=1, source_target_pairs={{0,1},{1,0},{2,3},{3,2},{4,5},{5,4},{6,7},{7,6},{8,9},{9,8},{10,11... | collective-permute-start | bytes 786440 | tf_op jit(solution)/shard_map/ppermute | solution.py:178
  14.4 0.0 copy-done.5
  14.4 0.0 collective-permute-done.2
  14.4 0.1 collective-permute-start.1
  14.5 0.1 collective-permute-done.8.ra_ref
  14.6 0.4 collective-permute-start.9
  15.0 0.1 collective-permute-done.4
  15.1 0.0 copy-done.2
  15.1 5.9 %prepare.1 = (bf16[4,2048,512]{2,1,0:T(8,128)(2,1)S(1)}, bf16[4,576,2048]{2,1,0:T(8,128)(2,1)S(1)}) custom-call(s32[4,16]{1,0:T(4,128)S(1)} %copy-done.2, f32[4,5,64]{2,1,0:T(8,128)S(1)} %pad_maximum_fusion.scale_ref, bf16[4,2048,512]{2,1,0:T(8,128)(2,1)} %latent_hbm.1, bf16[4,64,2048]{2,1,0:T(8,128)(2,1)} %rope_hbm.1), custom_call_target="tpu_custom_call" | custom-call | flops 20000000 | bytes 20000000 | tf_op jit(solution)/shard_map/prepare/pallas_call | solution.py:65
  21.0 0.0 collective-permute-done.9.rb_ref
  21.0 0.0 collective-permute-done.7.qb_ref
  21.0 4.3 %attend.3 = (bf16[4,64,512]{2,1,0:T(8,128)(2,1)S(1)}, bf16[4,64,512]{2,1,0:T(8,128)(2,1)S(1)}, f32[4,1,64]{2,1,0:T(1,128)S(1)}, f32[4,1,64]{2,1,0:T(1,128)S(1)}) custom-call(s32[4]{0:T(128)S(1)} %add_subtract_fusion.limit_ref, bf16[4,64,512]{2,1,0:T(8,128)(2,1)S(1)} %collective-permute-done.6.qa_ref, bf16[4,64,512]{2,1,0:T(8,128)(2,1)S(1)} %collective-permute-done.7.qb_ref, ...), custom_call_target="tpu_custom_call" | custom-call | flops 2281701376 | bytes 8388608 | tf_op jit(solution)/shard_map/attend/pallas_call | solution.py:138
  25.3 0.2 collective-permute-start.13
  25.4 0.4 collective-permute-start.10
  25.8 0.0 collective-permute-done.1.rb_ref
  25.8 0.0 collective-permute-done.qb_ref
  25.8 4.3 %attend.2 = (bf16[4,64,512]{2,1,0:T(8,128)(2,1)S(1)}, bf16[4,64,512]{2,1,0:T(8,128)(2,1)S(1)}, f32[4,1,64]{2,1,0:T(1,128)S(1)}, f32[4,1,64]{2,1,0:T(1,128)S(1)}) custom-call(s32[4]{0:T(128)S(1)} %add_subtract_fusion.limit_ref, bf16[4,64,512]{2,1,0:T(8,128)(2,1)S(1)} %bitcast.36, bf16[4,64,512]{2,1,0:T(8,128)(2,1)S(1)} %collective-permute-done.qb_ref, ...), custom_call_target="tpu_custom_call" | custom-call | flops 2281701376 | bytes 8388608 | tf_op jit(solution)/shard_map/attend/pallas_call | solution.py:138
  30.1 0.2 collective-permute-start.12
  30.2 0.4 collective-permute-start.5
  30.6 0.0 collective-permute-done.10
  30.6 1.8 %collective-permute-start.11 = (f32[4,1,64]{2,1,0:T(1,128)S(1)}, f32[4,1,64]{2,1,0:T(1,128)S(1)}, u32[]{:S(2)}, u32[]{:S(2)}) collective-permute-start(f32[4,1,64]{2,1,0:T(1,128)S(1)} %get-tuple-element.29), channel_id=1, source_target_pairs={{0,2},{1,3},{2,0},{3,1},{4,6},{5,7},{6,4},{7,5},{8,10},{9,11},{10,... | collective-permute-start | bytes 3080 | tf_op jit(solution)/shard_map/ppermute | solution.py:178
  32.4 0.0 collective-permute-done.13
  32.4 0.2 add_convert_fusion.1
  32.6 0.4 collective-permute-start.14
  33.0 0.0 collective-permute-done.5
  33.0 1.3 %collective-permute-done.11 = f32[4,1,64]{2,1,0:T(1,128)S(1)} collective-permute-done((f32[4,1,64]{2,1,0:T(1,128)S(1)}, f32[4,1,64]{2,1,0:T(1,128)S(1)}, u32[]{:S(2)}, u32[]{:S(2)}) %collective-permute-start.11) | collective-permute-done | bytes 1056 | tf_op jit(solution)/shard_map/ppermute | solution.py:178
  34.3 0.0 collective-permute-done.12
  34.3 6.4 %collective-permute-done.14 = bf16[4,64,512]{2,1,0:T(8,128)(2,1)S(1)} collective-permute-done((bf16[4,64,512]{2,1,0:T(8,128)(2,1)S(1)}, bf16[4,64,512]{2,1,0:T(8,128)(2,1)S(1)}, u32[]{:S(2)}, u32[]{:S(2)}) %collective-permute-start.14) | collective-permute-done | bytes 262176 | tf_op jit(solution)/shard_map/ppermute | solution.py:178
  40.8 0.2 add_convert_fusion
  41.0 0.0 copy-done.3
  41.0 0.7 %fusion.13 = bf16[4,2,32,128]{3,0,1,2:T(4,128)(2,1)S(1)} fusion(bf16[32,512,128]{2,1,0:T(8,128)(2,1)S(1)} %copy-done.3, bf16[4,2,32,512]{3,2,1,0:T(8,128)(2,1)S(1)} %bitcast.40), kind=kOutput, calls=%fused_computation.7 | convolution fusion | flops 33587200 | bytes 4521984 | tf_op jit(solution)/shard_map/rthc,hcv->rthv/dot_general | solution.py:214
  41.8 0.7 %copy.13 = bf16[4,2,32,128]{3,2,1,0:T(8,128)(2,1)} copy(bf16[4,2,32,128]{3,0,1,2:T(4,128)(2,1)S(1)} %fusion.13) | data formatting | bytes 131072 | tf_op jit(solution)/shard_map/convert_element_type | solution.py:215
  (8 shorter events, 0.1 us)
Async XLA Ops:
  0.0 0.8 %copy-start = (bf16[4,2,32,128]{3,2,1,0:T(8,128)(2,1)S(1)}, bf16[4,2,32,128]{3,2,1,0:T(8,128)(2,1)}, u32[]{:S(2)}) copy-start(bf16[4,2,32,128]{3,2,1,0:T(8,128)(2,1)} %param.9) | copy-start | bytes 196612
  0.0 6.8 %copy-start.4 = (f32[5,64]{1,0:T(8,128)S(1)}, f32[5,64]{1,0:T(8,128)}, u32[]{:S(2)}) copy-start(f32[5,64]{1,0:T(8,128)} %param.15) | copy-start | bytes 3844
  0.0 7.4 %copy-start.1 = (bf16[4,2,32,64]{3,2,1,0:T(8,128)(2,1)S(1)}, bf16[4,2,32,64]{3,2,1,0:T(8,128)(2,1)}, u32[]{:S(2)}) copy-start(bf16[4,2,32,64]{3,2,1,0:T(8,128)(2,1)} %param.10) | copy-start | bytes 98308
  0.0 14.4 %copy-start.5 = (s32[4]{0:T(128)S(1)}, s32[4]{0:T(128)}, u32[]{:S(2)}) copy-start(s32[4]{0:T(128)} %param.17) | copy-start | bytes 52
  0.0 15.1 %copy-start.2 = (s32[4,16]{1,0:T(4,128)S(1)}, s32[4,16]{1,0:T(4,128)}, u32[]{:S(2)}) copy-start(s32[4,16]{1,0:T(4,128)} %index_ref.1) | copy-start | bytes 772
  3.8 10.1 %collective-permute-start.6 = (bf16[4,64,512]{2,1,0:T(8,128)(2,1)S(1)}, bf16[4,64,512]{2,1,0:T(8,128)(2,1)S(1)}, u32[]{:S(2)}, u32[]{:S(2)}) collective-permute-start(bf16[4,64,512]{2,1,0:T(8,128)(2,1)S(1)} %bitcast.34), channel_id=1, source_target_pairs={{0,2},{1,3},{2,0},{3,1},{4,6},{5,7},{6,4},{7,5},{8,10},{9,11},{10,... | collective-permute-start | bytes 786440 | tf_op jit(solution)/shard_map/ppermute | solution.py:178
  6.8 7.1 %collective-permute-start.3 = (f32[5,64]{1,0:T(8,128)S(1)}, f32[5,64]{1,0:T(8,128)S(1)}, u32[]{:S(2)}, u32[]{:S(2)}) collective-permute-start(f32[5,64]{1,0:T(8,128)S(1)} %copy-done.4), channel_id=1, source_target_pairs={{0,2},{1,3},{2,0},{3,1},{4,6},{5,7},{6,4},{7,5},{8,10},{9,11},{10,... | collective-permute-start | bytes 3848 | tf_op jit(solution)/shard_map/ppermute | solution.py:178
  6.9 7.5 %collective-permute-start.2 = (f32[5,64]{1,0:T(8,128)S(1)}, f32[5,64]{1,0:T(8,128)S(1)}, u32[]{:S(2)}, u32[]{:S(2)}) collective-permute-start(f32[5,64]{1,0:T(8,128)S(1)} %copy-done.4), channel_id=1, source_target_pairs={{0,1},{1,0},{2,3},{3,2},{4,5},{5,4},{6,7},{7,6},{8,9},{9,8},{10,11... | collective-permute-start | bytes 3848 | tf_op jit(solution)/shard_map/ppermute | solution.py:178
  6.9 18.9 %collective-permute-start = (bf16[4,64,512]{2,1,0:T(8,128)(2,1)S(1)}, bf16[4,64,512]{2,1,0:T(8,128)(2,1)S(1)}, u32[]{:S(2)}, u32[]{:S(2)}) collective-permute-start(bf16[4,64,512]{2,1,0:T(8,128)(2,1)S(1)} %bitcast.35), channel_id=1, source_target_pairs={{0,1},{1,0},{2,3},{3,2},{4,5},{5,4},{6,7},{7,6},{8,9},{9,8},{10,11... | collective-permute-start | bytes 786440 | tf_op jit(solution)/shard_map/ppermute | solution.py:178
  7.4 7.2 %collective-permute-start.8 = (bf16[4,64,64]{2,1,0:T(8,128)(2,1)S(1)}, bf16[4,64,64]{2,1,0:T(8,128)(2,1)S(1)}, u32[]{:S(2)}, u32[]{:S(2)}) collective-permute-start(bf16[4,64,64]{2,1,0:T(8,128)(2,1)S(1)} %bitcast.37), channel_id=1, source_target_pairs={{0,2},{1,3},{2,0},{3,1},{4,6},{5,7},{6,4},{7,5},{8,10},{9,11},{10,... | collective-permute-start | bytes 98312 | tf_op jit(solution)/shard_map/ppermute | solution.py:178
  13.9 1.2 %collective-permute-start.4 = (f32[5,64]{1,0:T(8,128)S(1)}, f32[5,64]{1,0:T(8,128)S(1)}, u32[]{:S(2)}, u32[]{:S(2)}) collective-permute-start(f32[5,64]{1,0:T(8,128)S(1)} %collective-permute-done.3), channel_id=1, source_target_pairs={{0,1},{1,0},{2,3},{3,2},{4,5},{5,4},{6,7},{7,6},{8,9},{9,8},{10,11... | collective-permute-start | bytes 3848 | tf_op jit(solution)/shard_map/ppermute | solution.py:178
  13.9 7.1 %collective-permute-start.7 = (bf16[4,64,512]{2,1,0:T(8,128)(2,1)S(1)}, bf16[4,64,512]{2,1,0:T(8,128)(2,1)S(1)}, u32[]{:S(2)}, u32[]{:S(2)}) collective-permute-start(bf16[4,64,512]{2,1,0:T(8,128)(2,1)S(1)} %collective-permute-done.6.qa_ref), channel_id=1, source_target_pairs={{0,1},{1,0},{2,3},{3,2},{4,5},{5,4},{6,7},{7,6},{8,9},{9,8},{10,11... | collective-permute-start | bytes 786440 | tf_op jit(solution)/shard_map/ppermute | solution.py:178
  14.4 11.4 %collective-permute-start.1 = (bf16[4,64,64]{2,1,0:T(8,128)(2,1)S(1)}, bf16[4,64,64]{2,1,0:T(8,128)(2,1)S(1)}, u32[]{:S(2)}, u32[]{:S(2)}) collective-permute-start(bf16[4,64,64]{2,1,0:T(8,128)(2,1)S(1)} %bitcast.38), channel_id=1, source_target_pairs={{0,1},{1,0},{2,3},{3,2},{4,5},{5,4},{6,7},{7,6},{8,9},{9,8},{10,11... | collective-permute-start | bytes 98312 | tf_op jit(solution)/shard_map/ppermute | solution.py:178
  14.6 6.4 %collective-permute-start.9 = (bf16[4,64,64]{2,1,0:T(8,128)(2,1)S(1)}, bf16[4,64,64]{2,1,0:T(8,128)(2,1)S(1)}, u32[]{:S(2)}, u32[]{:S(2)}) collective-permute-start(bf16[4,64,64]{2,1,0:T(8,128)(2,1)S(1)} %collective-permute-done.8.ra_ref), channel_id=1, source_target_pairs={{0,1},{1,0},{2,3},{3,2},{4,5},{5,4},{6,7},{7,6},{8,9},{9,8},{10,11... | collective-permute-start | bytes 98312 | tf_op jit(solution)/shard_map/ppermute | solution.py:178
  25.3 7.1 %collective-permute-start.13 = (bf16[4,64,512]{2,1,0:T(8,128)(2,1)S(1)}, bf16[4,64,512]{2,1,0:T(8,128)(2,1)S(1)}, u32[]{:S(2)}, u32[]{:S(2)}) collective-permute-start(bf16[4,64,512]{2,1,0:T(8,128)(2,1)S(1)} %get-tuple-element.24), channel_id=1, source_target_pairs={{0,1},{1,0},{2,3},{3,2},{4,5},{5,4},{6,7},{7,6},{8,9},{9,8},{10,11... | collective-permute-start | bytes 786440 | tf_op jit(solution)/shard_map/ppermute | solution.py:178
  25.4 15.6 %copy-start.3 = (bf16[32,512,128]{2,1,0:T(8,128)(2,1)S(1)}, bf16[32,512,128]{2,1,0:T(8,128)(2,1)}, u32[]{:S(2)}) copy-start(bf16[32,512,128]{2,1,0:T(8,128)(2,1)} %param.12) | copy-start | bytes 12582916
  25.4 5.2 %collective-permute-start.10 = (f32[4,1,64]{2,1,0:T(1,128)S(1)}, f32[4,1,64]{2,1,0:T(1,128)S(1)}, u32[]{:S(2)}, u32[]{:S(2)}) collective-permute-start(f32[4,1,64]{2,1,0:T(1,128)S(1)} %get-tuple-element.21), channel_id=1, source_target_pairs={{0,1},{1,0},{2,3},{3,2},{4,5},{5,4},{6,7},{7,6},{8,9},{9,8},{10,11... | collective-permute-start | bytes 3080 | tf_op jit(solution)/shard_map/ppermute | solution.py:178
  30.1 4.3 %collective-permute-start.12 = (bf16[4,64,512]{2,1,0:T(8,128)(2,1)S(1)}, bf16[4,64,512]{2,1,0:T(8,128)(2,1)S(1)}, u32[]{:S(2)}, u32[]{:S(2)}) collective-permute-start(bf16[4,64,512]{2,1,0:T(8,128)(2,1)S(1)} %get-tuple-element.22), channel_id=1, source_target_pairs={{0,1},{1,0},{2,3},{3,2},{4,5},{5,4},{6,7},{7,6},{8,9},{9,8},{10,11... | collective-permute-start | bytes 786440 | tf_op jit(solution)/shard_map/ppermute | solution.py:178
  30.2 2.7 %collective-permute-start.5 = (f32[4,1,64]{2,1,0:T(1,128)S(1)}, f32[4,1,64]{2,1,0:T(1,128)S(1)}, u32[]{:S(2)}, u32[]{:S(2)}) collective-permute-start(f32[4,1,64]{2,1,0:T(1,128)S(1)} %get-tuple-element.19), channel_id=1, source_target_pairs={{0,1},{1,0},{2,3},{3,2},{4,5},{5,4},{6,7},{7,6},{8,9},{9,8},{10,11... | collective-permute-start | bytes 3080 | tf_op jit(solution)/shard_map/ppermute | solution.py:178
  30.6 3.7 %collective-permute-start.11 = (f32[4,1,64]{2,1,0:T(1,128)S(1)}, f32[4,1,64]{2,1,0:T(1,128)S(1)}, u32[]{:S(2)}, u32[]{:S(2)}) collective-permute-start(f32[4,1,64]{2,1,0:T(1,128)S(1)} %get-tuple-element.29), channel_id=1, source_target_pairs={{0,2},{1,3},{2,0},{3,1},{4,6},{5,7},{6,4},{7,5},{8,10},{9,11},{10,... | collective-permute-start | bytes 3080 | tf_op jit(solution)/shard_map/ppermute | solution.py:178
  32.6 8.2 %collective-permute-start.14 = (bf16[4,64,512]{2,1,0:T(8,128)(2,1)S(1)}, bf16[4,64,512]{2,1,0:T(8,128)(2,1)S(1)}, u32[]{:S(2)}, u32[]{:S(2)}) collective-permute-start(bf16[4,64,512]{2,1,0:T(8,128)(2,1)S(1)} %add_convert_fusion.1), channel_id=1, source_target_pairs={{0,2},{1,3},{2,0},{3,1},{4,6},{5,7},{6,4},{7,5},{8,10},{9,11},{10,... | collective-permute-start | bytes 786440 | tf_op jit(solution)/shard_map/ppermute | solution.py:178
